TPU v7x, 32 devices: a whole 2x2x4 slice. The times are simulated.
32 devices in a mesh: chan: 16 (over z, x, core), tm: 2 (over y).
Axes of the slice: x: 2, y: 2, z: 4, core: 2. Of those that a mesh axis runs over, the one named last changes fastest.
Arguments:
- samples: bfloat16 [2, 256, 32, 1024], P(None, 'chan', 'tm'), may hold values from -64 to 64
- steer_index: int32 [256, 256], replicated, may hold values from 0 to 255
Outputs:
- beams: bfloat16 [2, 128, 256, 32], P(None, 'chan', None, 'tm')
All inputs are finite; a program needn't handle non-finite values.
Results may differ from a plain program's by a relative error of at most 0.0081.
Values may be sent and summed in bfloat16 or wider, within the bound.
A program may use at most 128 MiB of HBM per device.

v0:
```python
import math

import jax
import jax.numpy as jnp
from jax import lax
from jax.sharding import PartitionSpec as P

C = 1024
PHASES = 256
CH_DEV = 8
ITERS = 3


HIGHEST = lax.Precision.HIGHEST


def transform_table(channels_all):
    offset = (C - channels_all) // 2
    channel_number = jnp.arange(channels_all, dtype=jnp.int32) + offset
    sample_number = jnp.arange(C, dtype=jnp.int32)
    phase_turns = channel_number[:, None] * sample_number[None, :] % C
    phase_angle = 2.0 * math.pi / C * phase_turns.astype(jnp.float32)
    window_taper = (
        0.5 - 0.5 * jnp.cos(2.0 * math.pi / C * sample_number.astype(jnp.float32))
    ) / math.sqrt(C)
    cosine = window_taper[None, :] * jnp.cos(phase_angle)
    sine_part = window_taper[None, :] * jnp.sin(phase_angle)
    coefficients = jnp.stack(
        [jnp.stack([cosine, sine_part], 1), jnp.stack([-sine_part, cosine], 1)], 0
    )
    return coefficients.astype(jnp.bfloat16)


def complex_product(left_real, left_imag, right_real, right_imag):
    real_part = jnp.dot(left_real, right_real, precision=HIGHEST) - jnp.dot(
        left_imag, right_imag, precision=HIGHEST
    )
    imag_part = jnp.dot(left_real, right_imag, precision=HIGHEST) + jnp.dot(
        left_imag, right_real, precision=HIGHEST
    )
    return (real_part, imag_part)


def invert_loaded(covariance_real, covariance_imag):
    matrix_order = covariance_real.shape[0]
    loading = 0.1 * jnp.mean(jnp.diagonal(covariance_real))
    identity = jnp.eye(matrix_order, dtype=jnp.float32)
    loaded = covariance_real + loading * identity
    magnitude = jnp.sqrt(loaded * loaded + covariance_imag * covariance_imag)
    largest = jnp.max(jnp.sum(magnitude, axis=1))

    def iterate(counter, state):
        approx_real, approx_imag = state
        image_real, image_imag = complex_product(loaded, covariance_imag, approx_real, approx_imag)
        square_real, square_imag = complex_product(approx_real, approx_imag, image_real, image_imag)
        return (2.0 * approx_real - square_real, 2.0 * approx_imag - square_imag)

    start_state = (identity / largest, jnp.zeros_like(identity))
    return lax.fori_loop(0, ITERS, iterate, start_state)


def form_weights(covariance_real, covariance_imag, steer_real, steer_imag):
    inverse_real, inverse_imag = invert_loaded(covariance_real, covariance_imag)
    gain_real, gain_imag = complex_product(inverse_real, inverse_imag, steer_real, steer_imag)
    response = jnp.sum(steer_real * gain_real + steer_imag * gain_imag, axis=0)
    factor = lax.rsqrt(response)
    return ((gain_real * factor).astype(jnp.bfloat16), (gain_imag * factor).astype(jnp.bfloat16))


def weights_stacked(covariance_real, covariance_imag, steer_real, steer_imag):
    weight_real, weight_imag = jax.vmap(form_weights, in_axes=(0, 0, None, None))(
        covariance_real, covariance_imag, steer_real, steer_imag
    )
    return jnp.stack([weight_real, weight_imag], 1)


def steering(steer_index):
    phase_angle = 2.0 * math.pi / PHASES * steer_index.astype(jnp.float32)
    return (jnp.cos(phase_angle).T, jnp.sin(phase_angle).T)


def apply_beams(weight_pair, spectrum):
    real_weight = weight_pair[:, 0]
    imag_weight = weight_pair[:, 1]
    beam_real = jnp.einsum(
        "knb,kns->kbs", real_weight, spectrum[0], preferred_element_type=jnp.float32
    ) + jnp.einsum("knb,kns->kbs", imag_weight, spectrum[1], preferred_element_type=jnp.float32)
    beam_imag = jnp.einsum(
        "knb,kns->kbs", real_weight, spectrum[1], preferred_element_type=jnp.float32
    ) - jnp.einsum("knb,kns->kbs", imag_weight, spectrum[0], preferred_element_type=jnp.float32)
    return jnp.stack([beam_real, beam_imag], 0).astype(jnp.bfloat16)


def local(samples, steer_index):
    channels_all = CH_DEV * lax.axis_size("chan")
    coefficients = transform_table(channels_all)
    spectra = lax.dot_general(
        coefficients, samples, (((2, 3), (0, 3)), ((), ())), preferred_element_type=jnp.float32
    ).astype(jnp.bfloat16)
    steer_real, steer_imag = steering(steer_index)
    turned = lax.all_to_all(
        lax.all_to_all(spectra, "chan", split_axis=1, concat_axis=2, tiled=True),
        "tm",
        split_axis=1,
        concat_axis=3,
        tiled=True,
    )
    outer_sums = jnp.einsum("ikns,jkms->kinjm", turned, turned, preferred_element_type=jnp.float32)
    snapshots = turned.shape[3]
    covariance_real = (outer_sums[:, 0, :, 0, :] + outer_sums[:, 1, :, 1, :]) / snapshots
    covariance_imag = (outer_sums[:, 1, :, 0, :] - outer_sums[:, 0, :, 1, :]) / snapshots
    weight_pair = weights_stacked(covariance_real, covariance_imag, steer_real, steer_imag)
    local_beams = apply_beams(weight_pair, turned)
    return lax.all_to_all(local_beams, "tm", split_axis=3, concat_axis=1, tiled=True)


def solution(mesh):
    return jax.shard_map(
        local,
        mesh=mesh,
        in_specs=(P(None, "chan", "tm", None), P()),
        out_specs=P(None, "chan", None, "tm"),
        check_vma=False,
    )
```

profile of v0, /device:TPU:0, one launch (start us, length us, event | category | flops | bytes accessed | tf_op | source)
XLA Modules:
  0.0 132.5 jit_solution(3292117637441634505)
XLA Ops:
  0.1 2.5 %fusion.41 = (bf16[128,1,1024]{2,0,1:T(8,128)(2,1)S(1)}, bf16[128,1,1024]{2,0,1:T(8,128)(2,1)S(1)}, bf16[128,1,1024]{2,0,1:T(8,128)(2,1)S(1)}) fusion(s32[128]{0:T(128)S(1)} %iota_add_fusion, f32[1024]{0:T(1024)S(1)} %subtract_multiply_fusion), kind=kLoop, calls=%fused_computation.69 | loop fusion | flops 2621440 | bytes 791040 | tf_op jit(solution)/shard_map/convert.11
  7.6 7.4 %all-to-all-start = ((bf16[16,2,2048]{2,1,0:T(2,128)(2,1)}), bf16[16,2,2048]{2,1,0:T(2,128)(2,1)S(1)}, u32[]{:S(2)}, u32[]{:S(2)}) async-start(bf16[16,2,2048]{2,1,0:T(2,128)(2,1)} %reshape.230), calls=%async_computation | async-start | bytes 262144 | tf_op jit(solution)/shard_map/all_to_all | solution.py:102
  18.4 4.5 %all-to-all-done = bf16[16,2,2048]{2,1,0:T(2,128)(2,1)S(1)} async-done(((bf16[16,2,2048]{2,1,0:T(2,128)(2,1)}), bf16[16,2,2048]{2,1,0:T(2,128)(2,1)S(1)}, u32[]{:S(2)}, u32[]{:S(2)}) %all-to-all-start) | async-done | bytes 131104 | tf_op jit(solution)/shard_map/all_to_all | solution.py:102
  26.3 3.4 %all-to-all-start.1 = ((bf16[2,8,256,16]{2,3,0,1:T(8,128)(2,1)}), bf16[2,8,256,16]{2,3,0,1:T(8,128)(2,1)S(1)}, u32[]{:S(2)}, u32[]{:S(2)}) async-start(bf16[2,8,256,16]{2,3,0,1:T(8,128)(2,1)} %reshape.229), calls=%async_computation.1 | async-start | bytes 262144 | tf_op jit(solution)/shard_map/all_to_all | solution.py:101
  29.7 4.4 %all-to-all-done.1 = bf16[2,8,256,16]{2,3,0,1:T(8,128)(2,1)S(1)} async-done(((bf16[2,8,256,16]{2,3,0,1:T(8,128)(2,1)}), bf16[2,8,256,16]{2,3,0,1:T(8,128)(2,1)S(1)}, u32[]{:S(2)}, u32[]{:S(2)}) %all-to-all-start.1) | async-done | bytes 131104 | tf_op jit(solution)/shard_map/all_to_all | solution.py:101
  37.1 16.5 %copy.116 = f32[4,256,256]{0,2,1:T(8,128)} copy(f32[4,256,256]{1,2,0:T(8,128)S(1)} %fusion.30) | data formatting | bytes 2097152 | tf_op jit(solution)/shard_map/div | solution.py:110
  53.6 2.3 %gather_fusion = f32[256,4]{1,0:T(8,128)S(1)} fusion(f32[4,256,256]{0,2,1:T(8,128)} %copy.116, s32[256]{0:T(256)S(1)} %bitcast.148), kind=kCustom, calls=%fused_computation | custom fusion | bytes 10240 | tf_op jit(solution)/shard_map/vmap(jit(diagonal))/cond/branch_0_fun/gather | solution.py:46
  56.0 3.8 %sqrt_reduce_fusion = (f32[4,256]{1,0:T(4,128)S(1)}, f32[4,256,256]{1,2,0:T(8,128)S(1)}, f32[4,256,256]{1,2,0:T(8,128)}) fusion(f32[256,256]{0,1:T(8,128)S(1)} %copy-done.3, f32[4]{0:T(128)S(1)} %broadcast_multiply_fusion, f32[4,2,256,2,256]{2,4,3,1,0:T(8,128)} %copy-done.1), kind=kLoop, calls=%fused_computation.52 | loop fusion | flops 2620416 | bytes 6557712 | tf_op jit(solution)/shard_map/vmap()/reduce_sum | solution.py:50
  61.9 51.7 %while.13 = (s32[]{:T(128)}, f32[4,256,256]{1,2,0:T(8,128)S(1)}, f32[4,256,256]{1,2,0:T(8,128)}, f32[4,256,256]{2,1,0:T(8,128)S(1)}, f32[4,256,256]{2,1,0:T(8,128)S(1)}, /*index=5*/s32[]{:T(128)}, s32[]{:T(128)}) while((s32[]{:T(128)}, f32[4,256,256]{1,2,0:T(8,128)S(1)}, f32[4,256,256]{1,2,0:T(8,128)}, ...), condition=%wide.region_4.5_spmd.clone, body=%wide.region_3.4_spmd.clone.sunk | while | flops 6445858816 | bytes 32505944 | solution.py:59
  62.1 2.1 %fusion.134 = f32[4,256,256]{2,1,0:T(8,128)} fusion(f32[4,256,256]{2,1,0:T(8,128)S(1)} %get-tuple-element.145, f32[4,256,256]{1,2,0:T(8,128)S(1)} %get-tuple-element.136), kind=kOutput, calls=%fused_computation.100.clone.1 | convolution fusion | flops 805306368 | bytes 3145728 | tf_op jit(solution)/shard_map/vmap()/while/body/eval_jaxpr/dot_general | solution.py:35
  65.5 2.4 %convolution_subtract_fusion.5 = f32[4,256,256]{2,1,0:T(8,128)S(1)} fusion(f32[4,256,256]{2,1,0:T(8,128)} %fusion.134, f32[4,256,256]{2,1,0:T(8,128)S(1)} %get-tuple-element.146, f32[4,256,256]{1,2,0:T(8,128)S(1)} %copy.170, pred[]{:T(512)S(6)} %compare.16), kind=kOutput, calls=%fused_computation.8.clone.1 | convolution fusion | flops 805830656 | bytes 4194305 | tf_op jit(solution)/shard_map/vmap()/while/body/eval_jaxpr/dot_general | solution.py:35
  74.1 2.3 %fusion.137 = f32[4,256,256]{1,2,0:T(8,128)S(1)} fusion(f32[4,256,256]{2,1,0:T(8,128)S(1)} %fusion.135, f32[4,256,256]{2,1,0:T(8,128)S(1)} %convolution_add_fusion.5, f32[4,256,256]{1,2,0:T(8,128)S(1)} %get-tuple-element.136, f32[4,256,256]{1,2,0:T(8,128)S(1)} %copy.170, pred[]{:T(512)S(6)} %compare.16), kind=kOutput, calls=%fused_computation.6.clone.1 | convolution fusion | flops 806354944 | bytes 5242881 | tf_op jit(solution)/shard_map/vmap()/while/body/eval_jaxpr/dot_general | solution.py:35
  76.4 2.9 %fusion.139 = f32[4,256,256]{1,2,0:T(8,128)} fusion(f32[4,256,256]{2,1,0:T(8,128)S(1)} %fusion.138, f32[4,256,256]{2,1,0:T(8,128)S(1)} %convolution_subtract_fusion.5, f32[4,256,256]{1,2,0:T(8,128)S(1)} %copy.170, pred[]{:T(512)S(6)} %compare.16), kind=kOutput, calls=%fused_computation.3.clone.1 | convolution fusion | flops 806617088 | bytes 4194305 | tf_op jit(solution)/shard_map/vmap()/while/body/eval_jaxpr/dot_general | solution.py:38
  82.7 2.4 %convolution_subtract_fusion.5 = f32[4,256,256]{2,1,0:T(8,128)S(1)} fusion(f32[4,256,256]{2,1,0:T(8,128)} %fusion.134, f32[4,256,256]{2,1,0:T(8,128)S(1)} %get-tuple-element.146, f32[4,256,256]{1,2,0:T(8,128)S(1)} %copy.170, pred[]{:T(512)S(6)} %compare.16), kind=kOutput, calls=%fused_computation.8.clone.1 | convolution fusion | flops 805830656 | bytes 4194305 | tf_op jit(solution)/shard_map/vmap()/while/body/eval_jaxpr/dot_general | solution.py:35
  91.3 2.3 %fusion.137 = f32[4,256,256]{1,2,0:T(8,128)S(1)} fusion(f32[4,256,256]{2,1,0:T(8,128)S(1)} %fusion.135, f32[4,256,256]{2,1,0:T(8,128)S(1)} %convolution_add_fusion.5, f32[4,256,256]{1,2,0:T(8,128)S(1)} %get-tuple-element.136, f32[4,256,256]{1,2,0:T(8,128)S(1)} %copy.170, pred[]{:T(512)S(6)} %compare.16), kind=kOutput, calls=%fused_computation.6.clone.1 | convolution fusion | flops 806354944 | bytes 5242881 | tf_op jit(solution)/shard_map/vmap()/while/body/eval_jaxpr/dot_general | solution.py:35
  93.5 2.9 %fusion.139 = f32[4,256,256]{1,2,0:T(8,128)} fusion(f32[4,256,256]{2,1,0:T(8,128)S(1)} %fusion.138, f32[4,256,256]{2,1,0:T(8,128)S(1)} %convolution_subtract_fusion.5, f32[4,256,256]{1,2,0:T(8,128)S(1)} %copy.170, pred[]{:T(512)S(6)} %compare.16), kind=kOutput, calls=%fused_computation.3.clone.1 | convolution fusion | flops 806617088 | bytes 4194305 | tf_op jit(solution)/shard_map/vmap()/while/body/eval_jaxpr/dot_general | solution.py:38
  99.8 2.4 %convolution_subtract_fusion.5 = f32[4,256,256]{2,1,0:T(8,128)S(1)} fusion(f32[4,256,256]{2,1,0:T(8,128)} %fusion.134, f32[4,256,256]{2,1,0:T(8,128)S(1)} %get-tuple-element.146, f32[4,256,256]{1,2,0:T(8,128)S(1)} %copy.170, pred[]{:T(512)S(6)} %compare.16), kind=kOutput, calls=%fused_computation.8.clone.1 | convolution fusion | flops 805830656 | bytes 4194305 | tf_op jit(solution)/shard_map/vmap()/while/body/eval_jaxpr/dot_general | solution.py:35
  108.4 2.3 %fusion.137 = f32[4,256,256]{1,2,0:T(8,128)S(1)} fusion(f32[4,256,256]{2,1,0:T(8,128)S(1)} %fusion.135, f32[4,256,256]{2,1,0:T(8,128)S(1)} %convolution_add_fusion.5, f32[4,256,256]{1,2,0:T(8,128)S(1)} %get-tuple-element.136, f32[4,256,256]{1,2,0:T(8,128)S(1)} %copy.170, pred[]{:T(512)S(6)} %compare.16), kind=kOutput, calls=%fused_computation.6.clone.1 | convolution fusion | flops 806354944 | bytes 5242881 | tf_op jit(solution)/shard_map/vmap()/while/body/eval_jaxpr/dot_general | solution.py:35
  110.7 2.9 %fusion.139 = f32[4,256,256]{1,2,0:T(8,128)} fusion(f32[4,256,256]{2,1,0:T(8,128)S(1)} %fusion.138, f32[4,256,256]{2,1,0:T(8,128)S(1)} %convolution_subtract_fusion.5, f32[4,256,256]{1,2,0:T(8,128)S(1)} %copy.170, pred[]{:T(512)S(6)} %compare.16), kind=kOutput, calls=%fused_computation.3.clone.1 | convolution fusion | flops 806617088 | bytes 4194305 | tf_op jit(solution)/shard_map/vmap()/while/body/eval_jaxpr/dot_general | solution.py:38
  113.7 2.5 %fusion.46 = f32[4,256,256]{2,1,0:T(8,128)S(1)} fusion(f32[4,256,256]{1,2,0:T(8,128)S(1)} %get-tuple-element.33, s32[256,256]{1,0:T(8,128)S(1)} %copy-done.2), kind=kOutput, calls=%fused_computation.74 | convolution fusion | flops 805437440 | bytes 2359296 | tf_op jit(solution)/shard_map/vmap()/dot_general | solution.py:35
  116.2 2.5 %fusion.42 = f32[4,256,256]{2,1,0:T(8,128)S(1)} fusion(f32[4,256,256]{1,2,0:T(8,128)S(1)} %get-tuple-element.33, s32[256,256]{1,0:T(8,128)S(1)} %copy-done.2), kind=kOutput, calls=%fused_computation.70 | convolution fusion | flops 805437440 | bytes 2359296 | tf_op jit(solution)/shard_map/vmap()/dot_general | solution.py:38
  118.7 2.6 %convolution_subtract_fusion.2 = f32[4,256,256]{2,1,0:T(8,128)S(1)} fusion(f32[4,256,256]{2,1,0:T(8,128)S(1)} %fusion.46, f32[4,256,256]{1,2,0:T(8,128)S(1)} %copy-done, s32[256,256]{1,0:T(8,128)S(1)} %copy-done.2), kind=kOutput, calls=%fused_computation.27 | convolution fusion | flops 805699584 | bytes 3407872 | tf_op jit(solution)/shard_map/vmap()/dot_general | solution.py:35
  121.3 2.6 %add_reduce_fusion = (f32[4,256]{1,0:T(4,128)S(1)}, f32[4,256,256]{2,1,0:T(8,128)S(1)}) fusion(f32[4,256,256]{2,1,0:T(8,128)S(1)} %convolution_subtract_fusion.2, f32[256,256]{1,0:T(8,128)S(1)} %copy-done.5, f32[256,256]{1,0:T(8,128)S(1)} %copy-done.4, f32[4,256,256]{2,1,0:T(8,128)S(1)} %fusion.42, f32[4,256,256]{1,2,0:T(8,128)S(1)} %copy-done, ...), kind=kOutput, calls=%fused_computation.51 | convolution fusion | flops 806747136 | bytes 4984832 | tf_op jit(solution)/shard_map/vmap()/dot_general | solution.py:38
  125.0 6.8 %all_to_all.54 = bf16[2,4,256,32]{2,1,0,3:T(4,128)(2,1)S(1)} all-to-all(bf16[2,4,256,32]{2,1,0,3:T(4,128)(2,1)S(1)} %copy.128), channel_id=1, replica_groups=mesh['chan'=16,'tm'=2] {'tm'}, dimensions={3} | all-to-all | bytes 262144 | tf_op jit(solution)/shard_map/all_to_all | solution.py:114
  (65 shorter events, 45.1 us)
Async XLA Ops:
  2.6 12.4 %copy-start.2 = (s32[256,256]{1,0:T(8,128)S(1)}, s32[256,256]{1,0:T(8,128)}, u32[]{:S(2)}) copy-start(s32[256,256]{1,0:T(8,128)} %param.5) | copy-start | bytes 786436
  7.6 15.3 %all-to-all-start = ((bf16[16,2,2048]{2,1,0:T(2,128)(2,1)}), bf16[16,2,2048]{2,1,0:T(2,128)(2,1)S(1)}, u32[]{:S(2)}, u32[]{:S(2)}) async-start(bf16[16,2,2048]{2,1,0:T(2,128)(2,1)} %reshape.230), calls=%async_computation | async-start | bytes 262144 | tf_op jit(solution)/shard_map/all_to_all | solution.py:102
  26.3 7.8 %all-to-all-start.1 = ((bf16[2,8,256,16]{2,3,0,1:T(8,128)(2,1)}), bf16[2,8,256,16]{2,3,0,1:T(8,128)(2,1)S(1)}, u32[]{:S(2)}, u32[]{:S(2)}) async-start(bf16[2,8,256,16]{2,3,0,1:T(8,128)(2,1)} %reshape.229), calls=%async_computation.1 | async-start | bytes 262144 | tf_op jit(solution)/shard_map/all_to_all | solution.py:101
  34.9 2.1 %copy-start.1 = (f32[4,2,256,2,256]{2,4,3,1,0:T(8,128)}, f32[4,2,256,2,256]{2,4,3,1,0:T(8,128)S(1)}, u32[]{:S(2)}) copy-start(f32[4,2,256,2,256]{2,4,3,1,0:T(8,128)S(1)} %fusion.73) | copy-start | bytes 12582916
  37.1 18.9 %copy-start.3 = (f32[256,256]{0,1:T(8,128)S(1)}, f32[256,256]{0,1:T(8,128)}, u32[]{:S(2)}) copy-start(f32[256,256]{0,1:T(8,128)} %fusion.48) | copy-start | bytes 786436
  113.7 5.0 %copy-start = (f32[4,256,256]{1,2,0:T(8,128)S(1)}, f32[4,256,256]{1,2,0:T(8,128)}, u32[]{:S(2)}) copy-start(f32[4,256,256]{1,2,0:T(8,128)} %get-tuple-element.34) | copy-start | bytes 3145732
  113.7 7.6 %copy-start.4 = (f32[256,256]{1,0:T(8,128)S(1)}, f32[256,256]{1,0:T(8,128)}, u32[]{:S(2)}) copy-start(f32[256,256]{1,0:T(8,128)} %copy.122) | copy-start | bytes 786436
  113.7 7.6 %copy-start.5 = (f32[256,256]{1,0:T(8,128)S(1)}, f32[256,256]{1,0:T(8,128)}, u32[]{:S(2)}) copy-start(f32[256,256]{1,0:T(8,128)} %copy.123) | copy-start | bytes 786436
where the time goes:
time: 133 us
  matrix products  61.2 us (46%)
  local copies, waits for them, and re-layouts  35.5 us (27%)
  starting transfers between devices  10.8 us (8%)
  waiting for transfers between devices  8.95 us (7%)
  other arithmetic  8.58 us (6%)
  blocking collectives  6.85 us (5%)
    dot_general x7, matrix products, complex_product(): jnp.dot(left_imag, right_imag, precision=HIGHEST)  16.6 us
    div x1, local copies, waits for them, and re-layouts, local(): (outer_sums[:, 0, :, 0, :] + outer_sums[:, 1, :, 1, :]) / snapshots  16.5 us
    dot_general x7, matrix products, complex_product(): jnp.dot(left_imag, right_real, precision=HIGHEST)  14.9 us
    dot_general x7, matrix products, complex_product(): jnp.dot(left_real, right_real, precision=HIGHEST)  14.6 us
    dot_general x7, matrix products, complex_product(): jnp.dot(left_real, right_imag, precision=HIGHEST)  11.8 us
    all_to_all x1, starting transfers between devices, local(): lax.all_to_all(spectra, 'chan', split_axis=1, concat_axis=2, tiled=True)  7.38 us
    all_to_all x1, blocking collectives, local(): lax.all_to_all(local_beams, 'tm', split_axis=3, concat_axis=1, tiled=True)  6.85 us
    unnamed x16, local copies, waits for them, and re-layouts  6.4 us
  transfers between devices with their start and end apart: 2, of which 2 were waited for; matrix products, arithmetic and copies ran while one was open for 3% of the time, Pallas kernels for 0%

commit v1 on v0

--- a/solution.py
+++ b/solution.py
@@ -1,17 +1,26 @@
+import functools
 import math
 
 import jax
 import jax.numpy as jnp
+import numpy as np
 from jax import lax
+from jax.experimental import pallas as pl
+from jax.experimental.pallas import tpu as pltpu
 from jax.sharding import PartitionSpec as P
 
 C = 1024
 PHASES = 256
 CH_DEV = 8
 ITERS = 3
+TERMS = 2**ITERS
+LANES = 128
 
 
 HIGHEST = lax.Precision.HIGHEST
+F32 = jnp.float32
+BF16 = jnp.bfloat16
+NT = (((1,), (1,)), ((), ()))
 
 
 def transform_table(channels_all):
@@ -114,9 +123,275 @@
     return lax.all_to_all(local_beams, "tm", split_axis=3, concat_axis=1, tiled=True)
 
 
+def taper_table(channels_all):
+    offset = (C - channels_all) // 2
+    channel = np.arange(channels_all) + offset
+    sample = np.arange(C)
+    angle = 2.0 * math.pi / C * (channel[None, :] * sample[:, None] % C)
+    taper = (0.5 - 0.5 * np.cos(2.0 * math.pi / C * sample)) / math.sqrt(C)
+    both = np.concatenate([taper[:, None] * np.cos(angle), taper[:, None] * np.sin(angle)], 1)
+    return both.astype(np.float32).astype(BF16)
+
+
+def iota(shape, axis):
+    return lax.broadcasted_iota(jnp.int32, shape, axis)
+
+
+def dot(a, b, dims=(((1,), (0,)), ((), ()))):
+    return lax.dot_general(a, b, dims, preferred_element_type=F32)
+
+
+def split(x):
+    high = x.astype(BF16)
+    return high, (x - high.astype(F32)).astype(BF16)
+
+
+def dot3(a, b):
+    (ah, al), (bh, bl) = a, b
+    return dot(ah, bh) + (dot(ah, bl) + dot(al, bh))
+
+
+def exchange_blocks(rows, count, width):
+    lane = iota(rows[0].shape, 1)
+    total = count * width
+    step = count // 2
+    while step:
+        low = (lane // width) & step == 0
+        done = list(rows)
+        for a in range(count):
+            if a & step:
+                continue
+            b = a + step
+            up = pltpu.roll(rows[b], step * width, 1)
+            down = pltpu.roll(rows[a], total - step * width, 1)
+            done[a] = jnp.where(low, rows[a], up)
+            done[b] = jnp.where(low, down, rows[b])
+        rows = done
+        step //= 2
+    return rows
+
+
+def steering_parts(index):
+    turn = index & (PHASES - 1)
+    quarter = PHASES // 4
+    quadrant = (turn + quarter // 2) // quarter
+    x = (turn - quarter * quadrant).astype(F32) * (2.0 * math.pi / PHASES)
+    y = x * x
+    s = x * (1.0 + y * (-1.0 / 6 + y * (1.0 / 120 + y * (-1.0 / 5040 + y * (1.0 / 362880)))))
+    c = 1.0 + y * (-0.5 + y * (1.0 / 24 + y * (-1.0 / 720 + y * (1.0 / 40320 - y * (1.0 / 3628800)))))
+    odd = quadrant & 1 == 1
+    flip_c = (quadrant + 1) & 2 == 2
+    flip_s = quadrant & 2 == 2
+    cosine = jnp.where(odd, s, c)
+    sine = jnp.where(odd, c, s)
+    return jnp.where(flip_c, -cosine, cosine), jnp.where(flip_s, -sine, sine)
+
+
+def fused(ni, nj, samples_ref, table_ref, index_ref, out_ref, re_ref, im_ref, send_ref, recv_ref,
+          steer_ref, x_ref, p_ref, send_sem, recv_sem):
+    nl, t_loc, q = 16, 16, 2 * CH_DEV
+    antennas = ni * nl
+    size = q * t_loc
+    devices = ni * nj
+    my_i, my_j = lax.axis_index("chan"), lax.axis_index("tm")
+    me = my_i * nj + my_j
+
+    barrier = pltpu.get_barrier_semaphore()
+
+    def greet(step, carry):
+        peer = lax.rem(me + step, devices)
+        pl.semaphore_signal(barrier, inc=1, device_id=(peer // nj, lax.rem(peer, nj)),
+                            device_id_type=pl.DeviceIdType.MESH)
+        return carry
+
+    lax.fori_loop(1, devices, greet, 0)
+
+    table = table_ref[...]
+    half = table.shape[1] // 2
+    first = dot(samples_ref[0], table)
+    second = dot(samples_ref[1], table)
+    re_ref[...] = first[:, :half] + second[:, half:]
+    im_ref[...] = second[:, :half] - first[:, half:]
+    parts = []
+    for ref in (re_ref, im_ref):
+        rows = [ref[pl.ds(t, nl, stride=t_loc), :] for t in range(t_loc)]
+        parts.append(exchange_blocks(rows, ni, CH_DEV))
+    blocks = jnp.concatenate(
+        [jnp.concatenate([a, b], 1) for a, b in zip(*parts)], 0
+    ).astype(BF16)
+    src, dst = iota((size, size), 0), iota((size, size), 1)
+    want = (dst // t_loc % 2) * (t_loc * CH_DEV) + (dst % t_loc) * CH_DEV + dst // (2 * t_loc)
+    order = jnp.where(src == want, 1.0, 0.0).astype(BF16)
+    send_ref[...] = dot(blocks, order).astype(BF16)
+
+    pl.semaphore_wait(barrier, devices - 1)
+
+    def copy_to(peer, slot):
+        to_i, to_j = peer // nj, lax.rem(peer, nj)
+        return pltpu.make_async_remote_copy(
+            src_ref=send_ref.at[pl.ds(pl.multiple_of(to_i * nl, nl), nl), :],
+            dst_ref=recv_ref.at[my_j, pl.ds(pl.multiple_of(my_i * nl, nl), nl), :],
+            send_sem=send_sem.at[slot],
+            recv_sem=recv_sem.at[me],
+            device_id=(to_i, to_j),
+            device_id_type=pl.DeviceIdType.MESH,
+        )
+
+    def send(step, carry):
+        copy_to(lax.rem(me + step, devices), step).start()
+        return carry
+
+    lax.fori_loop(1, devices, send, 0)
+    mine = pl.ds(pl.multiple_of(my_i * nl, nl), nl)
+    recv_ref[my_j, mine, :] = send_ref[mine, :]
+
+    cosine, sine = steering_parts(index_ref[...])
+    steer_ref[0], steer_ref[1] = split(cosine)
+    steer_ref[2], steer_ref[3] = split(sine)
+
+    def arrive(step, carry):
+        peer = lax.rem(me + step, devices)
+        from_i, from_j = peer // nj, lax.rem(peer, nj)
+        pltpu.make_async_remote_copy(
+            src_ref=send_ref.at[mine, :],
+            dst_ref=recv_ref.at[from_j, pl.ds(pl.multiple_of(from_i * nl, nl), nl), :],
+            send_sem=send_sem.at[step],
+            recv_sem=recv_sem.at[peer],
+            device_id=(from_i, from_j),
+            device_id_type=pl.DeviceIdType.MESH,
+        ).wait_recv()
+        return carry
+
+    lax.fori_loop(1, devices, arrive, 0)
+
+    groups = size // LANES
+    per = CH_DEV // groups
+    cols = nj * LANES
+    row_id, col_id = iota((cols, cols), 0), iota((cols, cols), 1)
+    chan_of = lambda x: x // (2 * t_loc) % per
+    same = chan_of(row_id) == chan_of(col_id)
+    on_diag = row_id == col_id
+    unit = jnp.where(on_diag, 1.0, 0.0).astype(BF16)
+    turn_j = jnp.where(row_id == (col_id ^ t_loc), jnp.where(col_id & t_loc == 0, 1.0, -1.0), 0.0).astype(BF16)
+    lane_chan = chan_of(iota((1, cols), 1))
+    span = 2 * t_loc
+    tiles = range(cols // span)
+
+    def by_channel(values):
+        return jnp.concatenate([jnp.broadcast_to(values[i % per], (span, cols)) for i in tiles], 0)
+
+    for g in range(groups):
+        z = jnp.concatenate([recv_ref[j, :, g * LANES : (g + 1) * LANES] for j in range(nj)], 1)
+        zt = dot(unit, z, NT).astype(BF16)
+        zj = dot(z, turn_j).astype(BF16)
+        zjt = jnp.concatenate(
+            [b for i in range(cols // span) for b in
+             (zt[i * span + t_loc : (i + 1) * span], -zt[i * span : i * span + t_loc])], 0)
+        gram = dot(zt, z) + dot(zjt, zj)
+        pt = (dot(zt, steer_ref[0], NT) + dot(zt, steer_ref[1], NT)) + (
+            dot(zjt, steer_ref[2], NT) + dot(zjt, steer_ref[3], NT))
+        diagonal = jnp.where(on_diag, gram, 0.0)
+        bounds, rhos = [], []
+        for k in range(per):
+            keep = jnp.where(lane_chan == k, 1.0, 0.0).astype(BF16)
+            cov_re = dot(z * keep, zt)
+            cov_im = dot(zj * keep, zt)
+            power = cov_re * cov_re + cov_im * cov_im
+            magnitude = power * lax.rsqrt(jnp.maximum(power, 1e-37))
+            largest = jnp.max(jnp.sum(magnitude, axis=0, keepdims=True), axis=1, keepdims=True)
+            trace = 0.0
+            for j in range(nj):
+                at = j * LANES + k * span
+                trace += jnp.sum(jnp.sum(diagonal[at : at + span], axis=0, keepdims=True), axis=1, keepdims=True)
+            load = (0.1 / antennas * 0.5) * trace
+            bound = largest + load
+            bounds.append(bound)
+            rhos.append(1.0 - load / bound)
+        sums = []
+        for k in range(per):
+            s, total = [], 1.0 + 0.0 * rhos[k]
+            for m in range(TERMS):
+                s.append(total)
+                total = 1.0 + rhos[k] * total
+            sums.append(s)
+        inverse = [1.0 / b for b in bounds]
+        x = jnp.where(same, gram, 0.0) * by_channel(inverse)
+        r1 = jnp.where(on_diag, by_channel(rhos), 0.0) - x
+        s1 = split(r1)
+        r2 = dot3(s1, s1)
+        s2 = split(r2)
+        r3 = dot3(s2, s1)
+        coef = lambda i: by_channel([sums[k][TERMS - 2 - i] for k in range(per)])
+        tail = jnp.where(on_diag, coef(3), 0.0) + coef(4) * r1 + coef(5) * r2 + coef(6) * r3
+        poly = (jnp.where(on_diag, coef(0), 0.0) + coef(1) * r1 + coef(2) * r2) + dot3(split(r3), split(tail))
+        vt = dot3(split(poly), split(pt))
+        product = pt * vt
+        x_ref[...] = x
+        p_ref[...] = pt
+        own = pl.ds(pl.multiple_of(my_j * LANES, LANES), LANES)
+        back = dot3(split(x_ref[own, :]), split(vt))
+        mine_p = p_ref[own, :]
+        for k in range(per):
+            at = k * span
+            energy = 0.0
+            for j in range(nj):
+                low = j * LANES + at
+                energy += jnp.sum(product[low : low + span], axis=0, keepdims=True)
+            whole = sums[k][TERMS - 1]
+            response = antennas * whole - energy * inverse[k]
+            factor = lax.rsqrt(response) * lax.rsqrt(bounds[k] * (1.0 / (nj * t_loc)))
+            beam = (whole * mine_p[at : at + span] - back[at : at + span]) * factor
+            beam = beam.astype(BF16)
+            out_ref[0, g * per + k] = beam[:t_loc]
+            out_ref[1, g * per + k] = beam[t_loc:]
+
+    def drain(step, carry):
+        copy_to(lax.rem(me + step, devices), step).wait_send()
+        return carry
+
+    lax.fori_loop(1, devices, drain, 0)
+
+
+def fused_local(ni, nj, samples, steer_index):
+    _, nl, t_loc, _ = samples.shape
+    beams, antennas = steer_index.shape
+    size = 2 * CH_DEV * t_loc
+    cols = nj * LANES
+    vmem = pl.BlockSpec(memory_space=pltpu.VMEM)
+    table = jnp.asarray(taper_table(CH_DEV * ni))
+    out = pl.pallas_call(
+        functools.partial(fused, ni, nj),
+        out_shape=jax.ShapeDtypeStruct((2, CH_DEV, t_loc, beams), BF16),
+        in_specs=[vmem] * 3,
+        out_specs=vmem,
+        scratch_shapes=[
+            pltpu.VMEM((nl * t_loc, CH_DEV * ni), F32),
+            pltpu.VMEM((nl * t_loc, CH_DEV * ni), F32),
+            pltpu.VMEM((antennas, size), BF16),
+            pltpu.VMEM((nj, antennas, size), BF16),
+            pltpu.VMEM((4, beams, antennas), BF16),
+            pltpu.VMEM((cols, cols), F32),
+            pltpu.VMEM((cols, beams), F32),
+            pltpu.SemaphoreType.DMA((ni * nj,)),
+            pltpu.SemaphoreType.DMA((ni * nj,)),
+        ],
+        compiler_params=pltpu.CompilerParams(collective_id=0, has_side_effects=True),
+    )(samples.reshape(2, nl * t_loc, C), table, steer_index)
+    return jnp.transpose(out, (0, 1, 3, 2))
+
+
+def choose(ni, nj, samples, steer_index):
+    _, nl, t_loc, _ = samples.shape
+    beams, antennas = steer_index.shape
+    tiled = nl == 16 and t_loc == 16 and CH_DEV * ni == LANES and antennas == nl * ni
+    if tiled and nj * LANES == antennas:
+        return fused_local(ni, nj, samples, steer_index)
+    return local(samples, steer_index)
+
+
 def solution(mesh):
     return jax.shard_map(
-        local,
+        functools.partial(choose, mesh.shape["chan"], mesh.shape["tm"]),
         mesh=mesh,
         in_specs=(P(None, "chan", "tm", None), P()),
         out_specs=P(None, "chan", None, "tm"),

time: 133 us -> 21.1 us (0.16)
  the two profiles are of different devices: /device:TPU:0 before, /device:TPU:15 now
where the time goes in v1:
time: 21.1 us; the launch traced here: 21 us
  Pallas kernels  19.4 us (92%)
  local copies, waits for them, and re-layouts  1.57 us (7%)
    pallas_call x1, Pallas kernels, fused_local(): pl.pallas_call(functools.partial(fused, ni, nj), out_shape=jax.ShapeDtype...  19.4 us
    unnamed x1, local copies, waits for them, and re-layouts  1.57 us

profile of v1, /device:TPU:15, one launch (start us, length us, event | category | flops | bytes accessed | tf_op | source)
XLA Modules:
  0.0 21.0 jit_solution(14966319432192825066)
XLA Ops:
  0.0 19.4 %shard_map.37 = bf16[2,8,16,256]{3,2,1,0:T(8,128)(2,1)} custom-call(bf16[2,256,1024]{2,1,0:T(8,128)(2,1)} %bitcast.2, bf16[1024,256]{1,0:T(8,128)(2,1)} %constant.2.clone.table_ref, s32[256,256]{1,0:T(8,128)} %index_ref.1), custom_call_target="tpu_custom_call" | custom-call | tf_op jit(solution)/shard_map/pallas_call | solution.py:362
  19.4 1.6 %copy.5 = bf16[2,8,256,16]{2,3,1,0:T(8,128)(2,1)} copy(bf16[2,8,256,16]{2,3,1,0:T(8,128)(2,1)} %bitcast.3) | data formatting | bytes 262144

commit v2 on v1

--- a/solution.py
+++ b/solution.py
@@ -187,8 +187,8 @@
     return jnp.where(flip_c, -cosine, cosine), jnp.where(flip_s, -sine, sine)
 
 
-def fused(ni, nj, samples_ref, table_ref, index_ref, out_ref, re_ref, im_ref, send_ref, recv_ref,
-          steer_ref, x_ref, p_ref, send_sem, recv_sem):
+def fused(ni, nj, samples_hbm, table_hbm, index_hbm, out_ref, samples_ref, table_ref, index_ref, re_ref, im_ref, send_ref, recv_ref,
+          steer_ref, x_ref, p_ref, load_sem, send_sem, recv_sem):
     nl, t_loc, q = 16, 16, 2 * CH_DEV
     antennas = ni * nl
     size = q * t_loc
@@ -198,17 +198,37 @@
 
     barrier = pltpu.get_barrier_semaphore()
 
-    def greet(step, carry):
-        peer = lax.rem(me + step, devices)
-        pl.semaphore_signal(barrier, inc=1, device_id=(peer // nj, lax.rem(peer, nj)),
+    def each_peer(body):
+        def around(step, carry):
+            ahead = my_i + step
+            peer_i = jnp.where(ahead >= ni, ahead - ni, ahead)
+            for peer_j in range(nj):
+                body(peer_i, peer_j, nj * step + peer_j)
+            return carry
+
+        for shift in range(1, nj):
+            ahead = my_j + shift
+            body(my_i, jnp.where(ahead >= nj, ahead - nj, ahead), shift - 1)
+        lax.fori_loop(1, ni, around, 0)
+
+    def greet(peer_i, peer_j, slot):
+        pl.semaphore_signal(barrier, inc=1, device_id=(peer_i, peer_j),
                             device_id_type=pl.DeviceIdType.MESH)
-        return carry
-
-    lax.fori_loop(1, devices, greet, 0)
-
+
+    each_peer(greet)
+
+    loads = [pltpu.make_async_copy(src, dst, load_sem.at[i]) for i, (src, dst) in enumerate(
+        [(table_hbm, table_ref), (samples_hbm.at[0], samples_ref.at[0]),
+         (samples_hbm.at[1], samples_ref.at[1]), (index_hbm, index_ref)])]
+    for load in loads:
+        load.start()
+
+    loads[0].wait()
     table = table_ref[...]
     half = table.shape[1] // 2
+    loads[1].wait()
     first = dot(samples_ref[0], table)
+    loads[2].wait()
     second = dot(samples_ref[1], table)
     re_ref[...] = first[:, :half] + second[:, half:]
     im_ref[...] = second[:, :half] - first[:, half:]
@@ -226,43 +246,38 @@
 
     pl.semaphore_wait(barrier, devices - 1)
 
-    def copy_to(peer, slot):
-        to_i, to_j = peer // nj, lax.rem(peer, nj)
+    rows_of = lambda i: pl.ds(pl.multiple_of(i * nl, nl), nl)
+
+    def copy_to(peer_i, peer_j, slot):
         return pltpu.make_async_remote_copy(
-            src_ref=send_ref.at[pl.ds(pl.multiple_of(to_i * nl, nl), nl), :],
-            dst_ref=recv_ref.at[my_j, pl.ds(pl.multiple_of(my_i * nl, nl), nl), :],
+            src_ref=send_ref.at[rows_of(peer_i), :],
+            dst_ref=recv_ref.at[my_j, rows_of(my_i), :],
             send_sem=send_sem.at[slot],
             recv_sem=recv_sem.at[me],
-            device_id=(to_i, to_j),
+            device_id=(peer_i, peer_j),
             device_id_type=pl.DeviceIdType.MESH,
         )
 
-    def send(step, carry):
-        copy_to(lax.rem(me + step, devices), step).start()
-        return carry
-
-    lax.fori_loop(1, devices, send, 0)
-    mine = pl.ds(pl.multiple_of(my_i * nl, nl), nl)
+    each_peer(lambda *peer: copy_to(*peer).start())
+    mine = rows_of(my_i)
     recv_ref[my_j, mine, :] = send_ref[mine, :]
 
+    loads[3].wait()
     cosine, sine = steering_parts(index_ref[...])
     steer_ref[0], steer_ref[1] = split(cosine)
     steer_ref[2], steer_ref[3] = split(sine)
 
-    def arrive(step, carry):
-        peer = lax.rem(me + step, devices)
-        from_i, from_j = peer // nj, lax.rem(peer, nj)
+    def arrive(peer_i, peer_j, slot):
         pltpu.make_async_remote_copy(
             src_ref=send_ref.at[mine, :],
-            dst_ref=recv_ref.at[from_j, pl.ds(pl.multiple_of(from_i * nl, nl), nl), :],
-            send_sem=send_sem.at[step],
-            recv_sem=recv_sem.at[peer],
-            device_id=(from_i, from_j),
+            dst_ref=recv_ref.at[peer_j, rows_of(peer_i), :],
+            send_sem=send_sem.at[slot],
+            recv_sem=recv_sem.at[peer_i * nj + peer_j],
+            device_id=(peer_i, peer_j),
             device_id_type=pl.DeviceIdType.MESH,
         ).wait_recv()
-        return carry
-
-    lax.fori_loop(1, devices, arrive, 0)
+
+    each_peer(arrive)
 
     groups = size // LANES
     per = CH_DEV // groups
@@ -345,11 +360,7 @@
             out_ref[0, g * per + k] = beam[:t_loc]
             out_ref[1, g * per + k] = beam[t_loc:]
 
-    def drain(step, carry):
-        copy_to(lax.rem(me + step, devices), step).wait_send()
-        return carry
-
-    lax.fori_loop(1, devices, drain, 0)
+    each_peer(lambda *peer: copy_to(*peer).wait_send())
 
 
 def fused_local(ni, nj, samples, steer_index):
@@ -361,10 +372,13 @@
     table = jnp.asarray(taper_table(CH_DEV * ni))
     out = pl.pallas_call(
         functools.partial(fused, ni, nj),
-        out_shape=jax.ShapeDtypeStruct((2, CH_DEV, t_loc, beams), BF16),
-        in_specs=[vmem] * 3,
+        out_shape=pltpu.VMEM((2, CH_DEV, t_loc, beams), BF16),
+        in_specs=[pl.BlockSpec(memory_space=pl.ANY)] * 3,
         out_specs=vmem,
         scratch_shapes=[
+            pltpu.VMEM((2, nl * t_loc, C), BF16),
+            pltpu.VMEM(table.shape, BF16),
+            pltpu.VMEM((beams, antennas), jnp.int32),
             pltpu.VMEM((nl * t_loc, CH_DEV * ni), F32),
             pltpu.VMEM((nl * t_loc, CH_DEV * ni), F32),
             pltpu.VMEM((antennas, size), BF16),
@@ -372,6 +386,7 @@
             pltpu.VMEM((4, beams, antennas), BF16),
             pltpu.VMEM((cols, cols), F32),
             pltpu.VMEM((cols, beams), F32),
+            pltpu.SemaphoreType.DMA((4,)),
             pltpu.SemaphoreType.DMA((ni * nj,)),
             pltpu.SemaphoreType.DMA((ni * nj,)),
         ],

time: 21.1 us -> 18.6 us (0.88)
  the two profiles are of different devices: /device:TPU:15 before, /device:TPU:1 now
where the time goes in v2:
time: 18.6 us; the launch traced here: 18.5 us
  Pallas kernels  17.8 us (96%)
  local copies, waits for them, and re-layouts  0.66 us (4%)
    pallas_call x1, Pallas kernels, fused_local(): pl.pallas_call(functools.partial(fused, ni, nj), out_shape=pltpu.VMEM((2,...  17.8 us
    unnamed x1, local copies, waits for them, and re-layouts  0.66 us

profile of v2, /device:TPU:1, one launch (start us, length us, event | category | flops | bytes accessed | tf_op | source)
XLA Modules:
  0.0 18.5 jit_solution(17245424037229106488)
XLA Ops:
  0.0 17.8 %shard_map.37 = bf16[2,8,16,256]{3,2,1,0:T(8,128)(2,1)S(1)} custom-call(bf16[2,256,1024]{2,1,0:T(8,128)(2,1)} %bitcast.3, bf16[1024,256]{1,0:T(8,128)(2,1)} %constant.2.clone.table_hbm, s32[256,256]{1,0:T(8,128)} %index_hbm.1), custom_call_target="tpu_custom_call" | custom-call | tf_op jit(solution)/shard_map/pallas_call | solution.py:373
  17.8 0.7 %copy.5 = bf16[2,8,256,16]{2,3,1,0:T(8,128)(2,1)} copy(bf16[2,8,256,16]{2,3,1,0:T(8,128)(2,1)S(1)} %bitcast.2) | data formatting | bytes 262144

commit v3 on v2

--- a/solution.py
+++ b/solution.py
@@ -1,4 +1,5 @@
 import functools
+import itertools
 import math
 
 import jax
@@ -187,35 +188,34 @@
     return jnp.where(flip_c, -cosine, cosine), jnp.where(flip_s, -sine, sine)
 
 
-def fused(ni, nj, samples_hbm, table_hbm, index_hbm, out_ref, samples_ref, table_ref, index_ref, re_ref, im_ref, send_ref, recv_ref,
-          steer_ref, x_ref, p_ref, load_sem, send_sem, recv_sem):
+def fused(ni, nj, samples_hbm, table_hbm, index_hbm, out_ref, samples_ref, table_ref, index_ref, re_ref,
+          im_ref, send_ref, recv_ref, steer_ref, load_sem, send_sem, recv_sem):
     nl, t_loc, q = 16, 16, 2 * CH_DEV
     antennas = ni * nl
     size = q * t_loc
-    devices = ni * nj
     my_i, my_j = lax.axis_index("chan"), lax.axis_index("tm")
-    me = my_i * nj + my_j
+    other_j = 1 - my_j
 
     barrier = pltpu.get_barrier_semaphore()
 
-    def each_peer(body):
-        def around(step, carry):
-            ahead = my_i + step
-            peer_i = jnp.where(ahead >= ni, ahead - ni, ahead)
-            for peer_j in range(nj):
-                body(peer_i, peer_j, nj * step + peer_j)
-            return carry
-
-        for shift in range(1, nj):
-            ahead = my_j + shift
-            body(my_i, jnp.where(ahead >= nj, ahead - nj, ahead), shift - 1)
-        lax.fori_loop(1, ni, around, 0)
-
-    def greet(peer_i, peer_j, slot):
+    def after(step):
+        ahead = my_i + step
+        return jnp.where(ahead >= ni, ahead - ni, ahead)
+
+    def around(body):
+        lax.fori_loop(1, ni, lambda step, carry: (body(step), carry)[1], 0)
+
+    def greet(peer_i, peer_j):
         pl.semaphore_signal(barrier, inc=1, device_id=(peer_i, peer_j),
                             device_id_type=pl.DeviceIdType.MESH)
 
-    each_peer(greet)
+    greet(my_i, other_j)
+
+    def greet_both(step):
+        greet(after(step), my_j)
+        greet(after(step), other_j)
+
+    around(greet_both)
 
     loads = [pltpu.make_async_copy(src, dst, load_sem.at[i]) for i, (src, dst) in enumerate(
         [(table_hbm, table_ref), (samples_hbm.at[0], samples_ref.at[0]),
@@ -244,70 +244,79 @@
     order = jnp.where(src == want, 1.0, 0.0).astype(BF16)
     send_ref[...] = dot(blocks, order).astype(BF16)
 
-    pl.semaphore_wait(barrier, devices - 1)
+    pl.semaphore_wait(barrier, ni * nj - 1)
 
     rows_of = lambda i: pl.ds(pl.multiple_of(i * nl, nl), nl)
-
-    def copy_to(peer_i, peer_j, slot):
+    mine = rows_of(my_i)
+
+    def block_copy(step, origin, plane):
+        peer = after(step)
         return pltpu.make_async_remote_copy(
-            src_ref=send_ref.at[rows_of(peer_i), :],
-            dst_ref=recv_ref.at[my_j, rows_of(my_i), :],
-            send_sem=send_sem.at[slot],
-            recv_sem=recv_sem.at[me],
-            device_id=(peer_i, peer_j),
+            src_ref=send_ref.at[rows_of(peer), :],
+            dst_ref=recv_ref.at[plane, rows_of(origin), :],
+            send_sem=send_sem.at[plane, step],
+            recv_sem=recv_sem.at[plane, origin],
+            device_id=(peer, other_j if plane else my_j),
             device_id_type=pl.DeviceIdType.MESH,
         )
 
-    each_peer(lambda *peer: copy_to(*peer).start())
-    mine = rows_of(my_i)
-    recv_ref[my_j, mine, :] = send_ref[mine, :]
+    def send(step):
+        block_copy(step, my_i, 0).start()
+        block_copy(step, my_i, 1).start()
+
+    block_copy(0, my_i, 1).start()
+    around(send)
+    recv_ref[0, mine, :] = send_ref[mine, :]
 
     loads[3].wait()
     cosine, sine = steering_parts(index_ref[...])
     steer_ref[0], steer_ref[1] = split(cosine)
     steer_ref[2], steer_ref[3] = split(sine)
 
-    def arrive(peer_i, peer_j, slot):
-        pltpu.make_async_remote_copy(
-            src_ref=send_ref.at[mine, :],
-            dst_ref=recv_ref.at[peer_j, rows_of(peer_i), :],
-            send_sem=send_sem.at[slot],
-            recv_sem=recv_sem.at[peer_i * nj + peer_j],
-            device_id=(peer_i, peer_j),
-            device_id_type=pl.DeviceIdType.MESH,
-        ).wait_recv()
-
-    each_peer(arrive)
+    span = 2 * t_loc
+    row_id, col_id = iota((size, size), 0), iota((size, size), 1)
+    on_diag = row_id == col_id
+    unit = jnp.where(on_diag, 1.0, 0.0).astype(BF16)
+    turn_j = jnp.where(row_id == (col_id ^ t_loc), jnp.where(col_id & t_loc == 0, 1.0, -1.0), 0.0).astype(BF16)
+
+    def prepare(plane):
+        z = recv_ref[plane]
+        zt = dot(unit, z, NT).astype(BF16)
+        zj = dot(z, turn_j).astype(BF16)
+        zjt = jnp.concatenate(
+            [b for i in range(size // span) for b in
+             (zt[i * span + t_loc : (i + 1) * span], -zt[i * span : i * span + t_loc])], 0)
+        pt = (dot(zt, steer_ref[0], NT) + dot(zt, steer_ref[1], NT)) + (
+            dot(zjt, steer_ref[2], NT) + dot(zjt, steer_ref[3], NT))
+        return z, zt, zj, zjt, pt
+
+    around(lambda step: block_copy(step, after(step), 0).wait_recv())
+    planes = [prepare(0)]
+    block_copy(0, my_i, 1).wait_recv()
+    around(lambda step: block_copy(step, after(step), 1).wait_recv())
+    planes.append(prepare(1))
 
     groups = size // LANES
     per = CH_DEV // groups
     cols = nj * LANES
-    row_id, col_id = iota((cols, cols), 0), iota((cols, cols), 1)
-    chan_of = lambda x: x // (2 * t_loc) % per
+    chan_of = lambda x: x // span % per
     same = chan_of(row_id) == chan_of(col_id)
-    on_diag = row_id == col_id
-    unit = jnp.where(on_diag, 1.0, 0.0).astype(BF16)
-    turn_j = jnp.where(row_id == (col_id ^ t_loc), jnp.where(col_id & t_loc == 0, 1.0, -1.0), 0.0).astype(BF16)
     lane_chan = chan_of(iota((1, cols), 1))
-    span = 2 * t_loc
-    tiles = range(cols // span)
 
     def by_channel(values):
-        return jnp.concatenate([jnp.broadcast_to(values[i % per], (span, cols)) for i in tiles], 0)
-
-    for g in range(groups):
-        z = jnp.concatenate([recv_ref[j, :, g * LANES : (g + 1) * LANES] for j in range(nj)], 1)
-        zt = dot(unit, z, NT).astype(BF16)
-        zj = dot(z, turn_j).astype(BF16)
-        zjt = jnp.concatenate(
-            [b for i in range(cols // span) for b in
-             (zt[i * span + t_loc : (i + 1) * span], -zt[i * span : i * span + t_loc])], 0)
+        return jnp.concatenate([jnp.broadcast_to(values[i % per], (span, cols)) for i in range(cols // span)], 0)
+
+    def group_steps(g):
+        cut = slice(g * LANES, (g + 1) * LANES)
+        z = jnp.concatenate([p[0][:, cut] for p in planes], 1)
+        zj = jnp.concatenate([p[2][:, cut] for p in planes], 1)
+        zt, zjt, pt = (jnp.concatenate([p[i][cut] for p in planes], 0) for i in (1, 3, 4))
         gram = dot(zt, z) + dot(zjt, zj)
-        pt = (dot(zt, steer_ref[0], NT) + dot(zt, steer_ref[1], NT)) + (
-            dot(zjt, steer_ref[2], NT) + dot(zjt, steer_ref[3], NT))
+        yield
         diagonal = jnp.where(on_diag, gram, 0.0)
         bounds, rhos = [], []
         for k in range(per):
+            yield
             keep = jnp.where(lane_chan == k, 1.0, 0.0).astype(BF16)
             cov_re = dot(z * keep, zt)
             cov_im = dot(zj * keep, zt)
@@ -322,6 +331,7 @@
             bound = largest + load
             bounds.append(bound)
             rhos.append(1.0 - load / bound)
+        yield
         sums = []
         for k in range(per):
             s, total = [], 1.0 + 0.0 * rhos[k]
@@ -333,19 +343,19 @@
         x = jnp.where(same, gram, 0.0) * by_channel(inverse)
         r1 = jnp.where(on_diag, by_channel(rhos), 0.0) - x
         s1 = split(r1)
+        yield
         r2 = dot3(s1, s1)
-        s2 = split(r2)
-        r3 = dot3(s2, s1)
+        yield
+        r3 = dot3(split(r2), s1)
         coef = lambda i: by_channel([sums[k][TERMS - 2 - i] for k in range(per)])
+        yield
         tail = jnp.where(on_diag, coef(3), 0.0) + coef(4) * r1 + coef(5) * r2 + coef(6) * r3
         poly = (jnp.where(on_diag, coef(0), 0.0) + coef(1) * r1 + coef(2) * r2) + dot3(split(r3), split(tail))
+        yield
         vt = dot3(split(poly), split(pt))
+        yield
         product = pt * vt
-        x_ref[...] = x
-        p_ref[...] = pt
-        own = pl.ds(pl.multiple_of(my_j * LANES, LANES), LANES)
-        back = dot3(split(x_ref[own, :]), split(vt))
-        mine_p = p_ref[own, :]
+        back = dot3(split(x[:LANES]), split(vt))
         for k in range(per):
             at = k * span
             energy = 0.0
@@ -355,19 +365,27 @@
             whole = sums[k][TERMS - 1]
             response = antennas * whole - energy * inverse[k]
             factor = lax.rsqrt(response) * lax.rsqrt(bounds[k] * (1.0 / (nj * t_loc)))
-            beam = (whole * mine_p[at : at + span] - back[at : at + span]) * factor
+            beam = (whole * pt[at : at + span] - back[at : at + span]) * factor
             beam = beam.astype(BF16)
             out_ref[0, g * per + k] = beam[:t_loc]
             out_ref[1, g * per + k] = beam[t_loc:]
 
-    each_peer(lambda *peer: copy_to(*peer).wait_send())
+    for _ in itertools.zip_longest(*[group_steps(g) for g in range(groups)]):
+        pass
+
+    block_copy(0, my_i, 1).wait_send()
+
+    def drain(step):
+        block_copy(step, my_i, 0).wait_send()
+        block_copy(step, my_i, 1).wait_send()
+
+    around(drain)
 
 
 def fused_local(ni, nj, samples, steer_index):
     _, nl, t_loc, _ = samples.shape
     beams, antennas = steer_index.shape
     size = 2 * CH_DEV * t_loc
-    cols = nj * LANES
     vmem = pl.BlockSpec(memory_space=pltpu.VMEM)
     table = jnp.asarray(taper_table(CH_DEV * ni))
     out = pl.pallas_call(
@@ -384,11 +402,9 @@
             pltpu.VMEM((antennas, size), BF16),
             pltpu.VMEM((nj, antennas, size), BF16),
             pltpu.VMEM((4, beams, antennas), BF16),
-            pltpu.VMEM((cols, cols), F32),
-            pltpu.VMEM((cols, beams), F32),
             pltpu.SemaphoreType.DMA((4,)),
-            pltpu.SemaphoreType.DMA((ni * nj,)),
-            pltpu.SemaphoreType.DMA((ni * nj,)),
+            pltpu.SemaphoreType.DMA((nj, ni)),
+            pltpu.SemaphoreType.DMA((nj, ni)),
         ],
         compiler_params=pltpu.CompilerParams(collective_id=0, has_side_effects=True),
     )(samples.reshape(2, nl * t_loc, C), table, steer_index)
@@ -399,7 +415,7 @@
     _, nl, t_loc, _ = samples.shape
     beams, antennas = steer_index.shape
     tiled = nl == 16 and t_loc == 16 and CH_DEV * ni == LANES and antennas == nl * ni
-    if tiled and nj * LANES == antennas:
+    if tiled and nj == 2:
         return fused_local(ni, nj, samples, steer_index)
     return local(samples, steer_index)
 

time: 18.6 us -> 17.3 us (0.930)
  Pallas kernels: 17.8 us -> 16.5 us
    pallas_call x1, Pallas kernels: 17.8 us -> 16.5 us  [fused_local(): pl.pallas_call(functools.partial(fused, ni, nj), out_shape=pltpu.VMEM((2,...]
where the time goes in v3:
time: 17.3 us; the launch traced here: 17.2 us
  Pallas kernels  16.5 us (95%)
  local copies, waits for them, and re-layouts  0.66 us (4%)
    pallas_call x1, Pallas kernels, fused_local(): pl.pallas_call(functools.partial(fused, ni, nj), out_shape=pltpu.VMEM((2,...  16.5 us
    unnamed x1, local copies, waits for them, and re-layouts  0.66 us

profile of v3, /device:TPU:1, one launch (start us, length us, event | category | flops | bytes accessed | tf_op | source)
XLA Modules:
  0.0 17.2 jit_solution(13400041644248942760)
XLA Ops:
  0.0 16.5 %shard_map.37 = bf16[2,8,16,256]{3,2,1,0:T(8,128)(2,1)S(1)} custom-call(bf16[2,256,1024]{2,1,0:T(8,128)(2,1)} %bitcast.3, bf16[1024,256]{1,0:T(8,128)(2,1)} %constant.2.clone.table_hbm, s32[256,256]{1,0:T(8,128)} %index_hbm.1), custom_call_target="tpu_custom_call" | custom-call | tf_op jit(solution)/shard_map/pallas_call | solution.py:391
  16.5 0.7 %copy.5 = bf16[2,8,256,16]{2,3,1,0:T(8,128)(2,1)} copy(bf16[2,8,256,16]{2,3,1,0:T(8,128)(2,1)S(1)} %bitcast.2) | data formatting | bytes 262144

commit v4 on v3

--- a/solution.py
+++ b/solution.py
@@ -254,8 +254,8 @@
         return pltpu.make_async_remote_copy(
             src_ref=send_ref.at[rows_of(peer), :],
             dst_ref=recv_ref.at[plane, rows_of(origin), :],
-            send_sem=send_sem.at[plane, step],
-            recv_sem=recv_sem.at[plane, origin],
+            send_sem=send_sem,
+            recv_sem=recv_sem.at[plane],
             device_id=(peer, other_j if plane else my_j),
             device_id_type=pl.DeviceIdType.MESH,
         )
@@ -290,10 +290,14 @@
             dot(zjt, steer_ref[2], NT) + dot(zjt, steer_ref[3], NT))
         return z, zt, zj, zjt, pt
 
-    around(lambda step: block_copy(step, after(step), 0).wait_recv())
+    def sized(ref, plane):
+        return pltpu.make_async_remote_copy(
+            src_ref=ref, dst_ref=ref, send_sem=send_sem, recv_sem=recv_sem.at[plane],
+            device_id=(my_i, other_j), device_id_type=pl.DeviceIdType.MESH)
+
+    sized(recv_ref.at[0, : antennas - nl], 0).wait_recv()
     planes = [prepare(0)]
-    block_copy(0, my_i, 1).wait_recv()
-    around(lambda step: block_copy(step, after(step), 1).wait_recv())
+    sized(recv_ref.at[1], 1).wait_recv()
     planes.append(prepare(1))
 
     groups = size // LANES
@@ -373,13 +377,8 @@
     for _ in itertools.zip_longest(*[group_steps(g) for g in range(groups)]):
         pass
 
-    block_copy(0, my_i, 1).wait_send()
-
-    def drain(step):
-        block_copy(step, my_i, 0).wait_send()
-        block_copy(step, my_i, 1).wait_send()
-
-    around(drain)
+    sized(send_ref.at[: antennas - nl], 0).wait_send()
+    sized(send_ref, 1).wait_send()
 
 
 def fused_local(ni, nj, samples, steer_index):
@@ -403,8 +402,8 @@
             pltpu.VMEM((nj, antennas, size), BF16),
             pltpu.VMEM((4, beams, antennas), BF16),
             pltpu.SemaphoreType.DMA((4,)),
-            pltpu.SemaphoreType.DMA((nj, ni)),
-            pltpu.SemaphoreType.DMA((nj, ni)),
+            pltpu.SemaphoreType.DMA,
+            pltpu.SemaphoreType.DMA((nj,)),
         ],
         compiler_params=pltpu.CompilerParams(collective_id=0, has_side_effects=True),
     )(samples.reshape(2, nl * t_loc, C), table, steer_index)

time: 17.3 us -> 16.7 us (0.965)
  Pallas kernels: 16.5 us -> 15.9 us
    pallas_call x1, Pallas kernels: 16.5 us -> 15.9 us  [fused_local(): pl.pallas_call(functools.partial(fused, ni, nj), out_shape=pltpu.VMEM((2,...]
where the time goes in v4:
time: 16.7 us; the launch traced here: 16.6 us
  Pallas kernels  15.9 us (95%)
  local copies, waits for them, and re-layouts  0.66 us (4%)
    pallas_call x1, Pallas kernels, fused_local(): pl.pallas_call(functools.partial(fused, ni, nj), out_shape=pltpu.VMEM((2,...  15.9 us
    unnamed x1, local copies, waits for them, and re-layouts  0.66 us

profile of v4, /device:TPU:1, one launch (start us, length us, event | category | flops | bytes accessed | tf_op | source)
XLA Modules:
  0.0 16.6 jit_solution(1972163848778727856)
XLA Ops:
  0.0 15.9 %shard_map.37 = bf16[2,8,16,256]{3,2,1,0:T(8,128)(2,1)S(1)} custom-call(bf16[2,256,1024]{2,1,0:T(8,128)(2,1)} %bitcast.3, bf16[1024,256]{1,0:T(8,128)(2,1)} %constant.2.clone.table_hbm, s32[256,256]{1,0:T(8,128)} %index_hbm.1), custom_call_target="tpu_custom_call" | custom-call | tf_op jit(solution)/shard_map/pallas_call | solution.py:390
  15.9 0.7 %copy.5 = bf16[2,8,256,16]{2,3,1,0:T(8,128)(2,1)} copy(bf16[2,8,256,16]{2,3,1,0:T(8,128)(2,1)S(1)} %bitcast.2) | data formatting | bytes 262144
